TPU v7x, 256 devices: a whole 4x4x8 slice. The times are simulated.
256 devices in a mesh: samples: 64 (over z, y, x_lo), vblocks: 4 (over x_hi, core).
Axes of the slice: x: 4 (x_hi: 2, x_lo: 2; x = x_hi * 2 + x_lo), y: 4, z: 8, core: 2. Of those that a mesh axis runs over, the one named last changes fastest.
Arguments:
- genotypes: int32 [65536, 4096], P('samples', 'vblocks'), may hold values from 0 to 2
- typed_mask: int32 [4096], P('vblocks'), may hold values 0 or 1
- z_scores: float32 [1024, 4096], P('samples', 'vblocks'), may hold values from -60 to 60
Outputs:
- solution: float32 [1024, 4096], P('samples', 'vblocks')
- imputed: float32 [1024, 4096], P('samples', 'vblocks')
All inputs are finite; a program needn't handle non-finite values. No bound on the sum of `typed_mask` on one device may be relied on, other than what follows from the above.
Results may differ from a plain program's by a relative error of at most 0.0068.
Values may be sent and summed in bfloat16 or wider, within the bound.
No kernel may reach another device: no remote copies, remote signals or barrier semaphores. Data moves between devices by JAX's collectives and lax.ppermute only.
A program may use at most 64 MiB of HBM per device.

v0:
```python
import jax
import jax.numpy as jnp
from jax import lax
from jax.sharding import Mesh, PartitionSpec as P

ITERS = 3
RIDGE = 0.1
EPSILON = 1e-05
HIGHEST = lax.Precision.HIGHEST
BF16 = jnp.bfloat16
F32 = jnp.float32
SAMPLE_AXES = ("z", "y", "xl")
BLOCK_AXES = ("xh", "core")
N_BLOCKS = 4


def from_next(block):
    return lax.ppermute(block, BLOCK_AXES, [(i + 1, i) for i in range(N_BLOCKS - 1)])


def from_previous(block):
    return lax.ppermute(block, BLOCK_AXES, [(i, i + 1) for i in range(N_BLOCKS - 1)])


def contract_rows(first_mat, second_mat):
    return lax.dot_general(
        first_mat, second_mat, (((0,), (0,)), ((), ())), preferred_element_type=F32
    )


def rounded(values):
    return lax.reduce_precision(values, exponent_bits=8, mantissa_bits=7)


def split3(vector):
    high = rounded(vector)
    rest = vector - high
    mid = rounded(rest)
    return jnp.concatenate([high, mid, rest - mid], axis=0).astype(BF16)


def join3(stacked):
    rows = stacked.shape[0] // 3
    return stacked[2 * rows :] + stacked[rows : 2 * rows] + stacked[:rows]


def times(vector, matrix, side):
    out = lax.dot_general(
        split3(vector), matrix, (((1,), (side,)), ((), ())), preferred_element_type=F32
    )
    return join3(out)


def gather_stats(local_sums, local_squares):
    sums, squares = (local_sums, local_squares)
    for axis in ("z", "y", "xl"):
        packed = jnp.concatenate([sums, squares], axis=0)[None]
        packed = lax.all_gather(packed, axis, axis=0, tiled=True)
        sums = packed[:, :-1].reshape(-1, packed.shape[-1])
        squares = jnp.sum(packed[:, -1], axis=0, keepdims=True)
    return (sums, squares)


def line_of(all_sums, all_squares, total_samples):
    coded_sum = jnp.sum(all_sums, axis=0, keepdims=True)
    mean_dosage = (coded_sum + total_samples) / total_samples
    squares = all_squares + 2.0 * coded_sum + total_samples
    variance = squares / total_samples - mean_dosage * mean_dosage
    scale = lax.rsqrt(variance + EPSILON)
    twos = 0.5 * (all_squares + coded_sum)
    zeros = 0.5 * (all_squares - coded_sum)
    ones = total_samples - all_squares
    level = rise = spread = 0.0
    for dosage, count in ((0.0, zeros), (1.0, ones), (2.0, twos)):
        away = dosage - mean_dosage
        value = rounded(away * scale)
        level = level + count * value
        rise = rise + count * value * away
        spread = spread + count * away * away
    slope = jnp.where(spread > 0.0, rise / jnp.where(spread > 0.0, spread, 1.0), scale)
    return (level / total_samples, slope)


def on_device(genotypes, typed_mask, z_scores):
    samples_dev, width = genotypes.shape
    n_dev = lax.axis_size(SAMPLE_AXES)
    total_samples = samples_dev * n_dev
    coded = (genotypes - 1).astype(BF16)
    following = from_next(coded)
    joined = jnp.concatenate([coded, following], axis=1)
    joined_f = joined.astype(F32)
    sums = jnp.sum(joined_f, axis=0, keepdims=True)
    squares = jnp.sum(joined_f * joined_f, axis=0, keepdims=True)
    counts = contract_rows(coded, joined)
    centred = (counts - sums[0, :width, None] * (sums / samples_dev)).astype(BF16)
    within = lax.psum_scatter(centred, "z", scatter_dimension=0, tiled=True)
    within = lax.psum_scatter(within.astype(F32), "y", scatter_dimension=0, tiled=True)
    within = lax.psum_scatter(within, "xl", scatter_dimension=0, tiled=True)
    all_sums, all_squares = gather_stats(sums, squares)
    level, slope = line_of(all_sums, all_squares, total_samples)
    off = (all_sums - jnp.mean(all_sums, axis=0, keepdims=True)) * slope
    rows = within.shape[0]
    start = lax.axis_index(SAMPLE_AXES) * rows
    off_rows = lax.dynamic_slice_in_dim(off, start, rows, axis=1)
    slope_rows = lax.dynamic_slice_in_dim(slope, start, rows, axis=1)
    level_rows = lax.dynamic_slice_in_dim(level, start, rows, axis=1)
    between = lax.dot_general(
        off_rows, off, (((0,), (0,)), ((), ())), precision=HIGHEST, preferred_element_type=F32
    )
    link = (within * slope * slope_rows[0][:, None] + between / samples_dev) / total_samples
    link = link + level_rows[0][:, None] * level
    link_rows = link.astype(BF16)
    gathered = lax.all_gather(link_rows, "xl", axis=0, tiled=True)
    gathered = lax.all_gather(gathered, "y", axis=0, tiled=True)
    gathered = lax.all_gather(gathered, "z", axis=0, tiled=True)
    own_block = gathered[:, :width]
    edge_block = gathered[:, width:]

    def apply_link(vector):
        ahead_part = from_next(vector)
        outgoing = times(vector, edge_block, 0)
        lower_part = from_previous(outgoing)
        result = times(vector, own_block, 1)
        result = result + 0.5 * times(ahead_part, edge_block, 1)
        return result + 0.5 * lower_part

    def dots(*pairs):
        local = jnp.stack([jnp.sum(a * b, axis=1) for a, b in pairs])
        return lax.psum(local, BLOCK_AXES)

    mask_row = typed_mask.astype(F32)[None, :]
    right_side = mask_row * z_scores
    residual = right_side
    linked = apply_link(mask_row * residual)
    image = mask_row * linked + RIDGE * residual
    norm_now, curvature = dots((residual, residual), (residual, image))
    direction = residual
    step_size = (norm_now / curvature)[:, None]
    solution = step_size * direction
    projected = step_size * linked
    for iteration in range(1, ITERS):
        residual = residual - step_size * image
        fresh_link = apply_link(mask_row * residual)
        fresh_image = mask_row * fresh_link + RIDGE * residual
        norm_next, fresh_curve, cross_a, cross_b, old_curve = dots(
            (residual, residual),
            (residual, fresh_image),
            (residual, image),
            (direction, fresh_image),
            (direction, image),
        )
        ratio = norm_next / norm_now
        curvature = fresh_curve + ratio * (cross_a + cross_b) + ratio * ratio * old_curve
        step_size = (norm_next / curvature)[:, None]
        direction = residual + ratio[:, None] * direction
        image = fresh_image + ratio[:, None] * image
        linked = fresh_link + ratio[:, None] * linked
        solution = solution + step_size * direction
        projected = projected + step_size * linked
        norm_now = norm_next
    imputed = jnp.where(typed_mask[None, :] == 1, z_scores, projected)
    return (solution, imputed)


def solution(mesh):
    fine = Mesh(mesh.devices.reshape(8, 4, 2, 2, 2), SAMPLE_AXES + BLOCK_AXES)
    placed = (P(SAMPLE_AXES, BLOCK_AXES), P(BLOCK_AXES), P(SAMPLE_AXES, BLOCK_AXES))
    return jax.shard_map(
        on_device,
        mesh=fine,
        in_specs=placed,
        out_specs=(P(SAMPLE_AXES, BLOCK_AXES), P(SAMPLE_AXES, BLOCK_AXES)),
        check_vma=False,
    )
```

profile of v0, /device:TPU:1, one launch (start us, length us, event | category | flops | bytes accessed | tf_op | source)
XLA Modules:
  0.0 291.5 jit_solution(16057749935253873127)
XLA Ops:
  7.2 0.0 reduce-scatter.4.cloned.1.call-start
  7.2 2.8 add_convert_fusion
  10.0 5.1 %collective-permute-start = (bf16[1024,1024]{1,0:T(8,128)(2,1)S(1)}, bf16[1024,1024]{1,0:T(8,128)(2,1)S(1)}, u32[]{:S(2)}, u32[]{:S(2)}) collective-permute-start(bf16[1024,1024]{1,0:T(8,128)(2,1)S(1)} %add_convert_fusion), channel_id=1, source_target_pairs={{1,0},{2,1},{3,2},{5,4},{6,5},{7,6},{9,8},{10,9},{11,10},{13,12},{... | collective-permute-start | bytes 6291464 | tf_op jit(solution)/shard_map/ppermute | solution.py:18
  15.1 24.6 %collective-permute-done = bf16[1024,1024]{1,0:T(8,128)(2,1)S(1)} collective-permute-done((bf16[1024,1024]{1,0:T(8,128)(2,1)S(1)}, bf16[1024,1024]{1,0:T(8,128)(2,1)S(1)}, u32[]{:S(2)}, u32[]{:S(2)}) %collective-permute-start) | collective-permute-done | bytes 2097184 | tf_op jit(solution)/shard_map/ppermute | solution.py:18
  39.7 1.4 convert_reduce_fusion
  41.1 6.5 %subtract_convert_fusion = bf16[1024,2048]{1,0:T(8,128)(2,1)} fusion(f32[2048]{0:T(1024)S(1)} %broadcast_multiply_fusion.3, f32[1024]{0:T(1024)S(1)} %bitcast.95, bf16[1024,1024]{1,0:T(8,128)(2,1)S(1)} %add_convert_fusion, bf16[1024,1024]{1,0:T(8,128)(2,1)S(1)} %collective-permute-done), kind=kOutput, calls=%fused_computation.3 | convolution fusion | flops 4309647360 | bytes 8400896 | tf_op jit(solution)/shard_map/dot_general | solution.py:26
  47.6 0.0 reduce-scatter.4.cloned.1.call-update
  47.6 0.0 reduce-scatter.6.cloned.1.call-start
  47.7 23.4 %all-gather.3 = f32[8,2,2048]{2,1,0:T(2,128)S(1)} all-gather(f32[1,2,2048]{2,1,0:T(2,128)S(1)} %maximum_bitcast_fusion.2), channel_id=2, replica_groups=mesh['z'=8,'y'=4,'xl'=2,'xh'=2,'core'=2] {'z'}, dimensions={0}, use_global_device_ids=true | all-gather | bytes 147456 | tf_op jit(solution)/shard_map/all_gather | solution.py:58
  71.1 0.1 fusion.90
  71.3 11.7 %all-gather.4 = f32[4,9,2048]{2,1,0:T(8,128)S(1)} all-gather(f32[1,9,2048]{2,1,0:T(8,128)S(1)} %maximum_bitcast_fusion.1), channel_id=3, replica_groups=mesh['z'=8,'y'=4,'xl'=2,'xh'=2,'core'=2] {'y'}, dimensions={0}, use_global_device_ids=true | all-gather | bytes 368640 | tf_op jit(solution)/shard_map/all_gather | solution.py:58
  83.0 21.1 %reduce-scatter.4.cloned.1.call-done = bf16[128,2048]{1,0:T(8,128)(2,1)} async-done(((bf16[1024,2048]{1,0:T(8,128)(2,1)}), bf16[128,2048]{1,0:T(8,128)(2,1)}) %reduce-scatter.4.cloned.1.call-update) | async-done | bytes 524304 | tf_op jit(solution)/shard_map/reduce_scatter | solution.py:96
  104.1 2.1 convert_element_type.31
  106.3 0.0 reduce-scatter.6.cloned.1.call-update
  106.3 0.0 reduce-scatter.8.cloned.1.call-start
  106.4 9.2 %all-gather.5 = f32[2,33,2048]{2,1,0:T(8,128)S(1)} all-gather(f32[1,33,2048]{2,1,0:T(8,128)S(1)} %maximum_bitcast_fusion), channel_id=4, replica_groups=mesh['z'=8,'y'=4,'xl'=2,'xh'=2,'core'=2] {'xl'}, dimensions={0}, use_global_device_ids=true | all-gather | bytes 811008 | tf_op jit(solution)/shard_map/all_gather | solution.py:58
  115.7 0.1 slice_reduce_fusion.3
  115.7 0.1 reduce-precision_multiply_fusion.1
  115.8 0.1 reduce-precision_multiply_fusion.2
  115.9 14.4 %reduce-scatter.6.cloned.1.call-done = f32[32,2048]{1,0:T(8,128)} async-done(((f32[128,2048]{1,0:T(8,128)}), f32[32,2048]{1,0:T(8,128)}) %reduce-scatter.6.cloned.1.call-update) | async-done | bytes 262160 | tf_op jit(solution)/shard_map/reduce_scatter | solution.py:97
  130.2 0.0 reduce-scatter.8.cloned.1.call-update
  130.3 0.0 all-gather.8.cloned.1.call-start
  130.3 0.1 fusion.75
  130.4 0.1 fusion.23
  130.5 20.2 %reduce-scatter.8.cloned.1.call-done = f32[16,2048]{1,0:T(8,128)} async-done(((f32[32,2048]{1,0:T(8,128)}), f32[16,2048]{1,0:T(8,128)}) %reduce-scatter.8.cloned.1.call-update) | async-done | bytes 131088 | tf_op jit(solution)/shard_map/reduce_scatter | solution.py:98
  150.6 1.4 fusion.4
  152.0 3.8 %all_gather.21 = bf16[32,2048]{1,0:T(8,128)(2,1)S(1)} all-gather(bf16[16,2048]{1,0:T(8,128)(2,1)S(1)} %fusion.4), channel_id=1, replica_groups=mesh['z'=8,'y'=4,'xl'=2,'xh'=2,'core'=2] {'xl'}, dimensions={0}, use_global_device_ids=true | all-gather | bytes 196608 | tf_op jit(solution)/shard_map/all_gather | solution.py:113
  155.8 11.5 %all_gather.22 = bf16[128,2048]{1,0:T(8,128)(2,1)} all-gather(bf16[32,2048]{1,0:T(8,128)(2,1)S(1)} %all_gather.21), channel_id=1, replica_groups=mesh['z'=8,'y'=4,'xl'=2,'xh'=2,'core'=2] {'y'}, dimensions={0}, use_global_device_ids=true | all-gather | bytes 655360 | tf_op jit(solution)/shard_map/all_gather | solution.py:114
  167.3 0.0 all-gather.8.cloned.1.call-update
  167.3 0.0 copy-done.1
  167.3 0.0 copy-done
  167.3 6.7 %collective-permute-start.1 = (f32[16,1024]{1,0:T(8,128)S(1)}, f32[16,1024]{1,0:T(8,128)S(1)}, u32[]{:S(2)}, u32[]{:S(2)}) collective-permute-start(f32[16,1024]{1,0:T(8,128)S(1)} %get-tuple-element.28), channel_id=1, source_target_pairs={{1,0},{2,1},{3,2},{5,4},{6,5},{7,6},{9,8},{10,9},{11,10},{13,12},{... | collective-permute-start | bytes 196616 | tf_op jit(solution)/shard_map/ppermute | solution.py:18
  174.1 4.2 %collective-permute-done.1 = f32[16,1024]{1,0:T(8,128)S(1)} collective-permute-done((f32[16,1024]{1,0:T(8,128)S(1)}, f32[16,1024]{1,0:T(8,128)S(1)}, u32[]{:S(2)}, u32[]{:S(2)}) %collective-permute-start.1) | collective-permute-done | bytes 65568 | tf_op jit(solution)/shard_map/ppermute | solution.py:18
  178.3 48.0 %all-gather.8.cloned.1.call-done = bf16[1024,2048]{1,0:T(8,128)(2,1)} async-done(((bf16[128,2048]{1,0:T(8,128)(2,1)}), bf16[1024,2048]{1,0:T(8,128)(2,1)}) %all-gather.8.cloned.1.call-update) | async-done | bytes 4194320 | tf_op jit(solution)/shard_map/all_gather | solution.py:115
  226.3 2.2 fusion.19
  228.6 5.3 %collective-permute-start.2 = (f32[16,1024]{1,0:T(8,128)S(1)}, f32[16,1024]{1,0:T(8,128)S(1)}, u32[]{:S(2)}, u32[]{:S(2)}) collective-permute-start(f32[16,1024]{1,0:T(8,128)S(1)} %slice_add_fusion.12), channel_id=1, source_target_pairs={{0,1},{1,2},{2,3},{4,5},{5,6},{6,7},{8,9},{9,10},{10,11},{12,13},{... | collective-permute-start | bytes 196616 | tf_op jit(solution)/shard_map/ppermute | solution.py:22
  233.9 2.3 fusion.9
  236.3 0.0 copy-done.2
  236.3 0.7 fusion.21
  237.0 0.0 collective-permute-done.2
  237.0 0.2 multiply_reduce_fusion.10
  237.2 6.6 %psum.21 = f32[2,16]{1,0:T(2,128)S(1)} all-reduce(f32[2,16]{1,0:T(2,128)S(1)} %pad_maximum_fusion.11), channel_id=1, replica_groups=mesh['z'=8,'y'=4,'xl'=2,'xh'=2,'core'=2] {'xh','core'}, use_global_device_ids=true, to_apply=%region_11.12 | all-reduce | flops 32 | bytes 256 | tf_op jit(solution)/shard_map/psum | solution.py:129
  243.8 0.1 reduce-precision_convert_fusion.7
  244.0 3.2 %collective-permute-start.3 = (f32[16,1024]{1,0:T(8,128)S(1)}, f32[16,1024]{1,0:T(8,128)S(1)}, u32[]{:S(2)}, u32[]{:S(2)}) collective-permute-start(f32[16,1024]{1,0:T(8,128)S(1)} %get-tuple-element.25), channel_id=1, source_target_pairs={{1,0},{2,1},{3,2},{5,4},{6,5},{7,6},{9,8},{10,9},{11,10},{13,12},{... | collective-permute-start | bytes 196616 | tf_op jit(solution)/shard_map/ppermute | solution.py:18
  247.2 2.1 fusion.15
  249.3 4.7 %collective-permute-start.4 = (f32[16,1024]{1,0:T(8,128)S(1)}, f32[16,1024]{1,0:T(8,128)S(1)}, u32[]{:S(2)}, u32[]{:S(2)}) collective-permute-start(f32[16,1024]{1,0:T(8,128)S(1)} %slice_add_fusion.6), channel_id=1, source_target_pairs={{0,1},{1,2},{2,3},{4,5},{5,6},{6,7},{8,9},{9,10},{10,11},{12,13},{... | collective-permute-start | bytes 196616 | tf_op jit(solution)/shard_map/ppermute | solution.py:22
  253.9 2.3 fusion.7
  256.3 0.0 collective-permute-done.3
  256.3 0.0 copy-done.3
  256.3 0.7 fusion.17
  257.1 0.0 collective-permute-done.4
  257.1 0.2 multiply_reduce_fusion.5
  257.4 6.6 %psum.22 = f32[5,16]{1,0:T(8,128)S(1)} all-reduce(f32[5,16]{1,0:T(8,128)S(1)} %stack.50), channel_id=1, replica_groups=mesh['z'=8,'y'=4,'xl'=2,'xh'=2,'core'=2] {'xh','core'}, use_global_device_ids=true, to_apply=%region_16.17 | all-reduce | flops 80 | bytes 640 | tf_op jit(solution)/shard_map/psum | solution.py:129
  264.0 0.1 reduce-precision_convert_fusion.3
  264.1 3.2 %collective-permute-start.5 = (f32[16,1024]{1,0:T(8,128)S(1)}, f32[16,1024]{1,0:T(8,128)S(1)}, u32[]{:S(2)}, u32[]{:S(2)}) collective-permute-start(f32[16,1024]{1,0:T(8,128)S(1)} %get-tuple-element.19), channel_id=1, source_target_pairs={{1,0},{2,1},{3,2},{5,4},{6,5},{7,6},{9,8},{10,9},{11,10},{13,12},{... | collective-permute-start | bytes 196616 | tf_op jit(solution)/shard_map/ppermute | solution.py:18
  267.4 2.1 fusion.11
  269.5 4.7 %collective-permute-start.6 = (f32[16,1024]{1,0:T(8,128)S(1)}, f32[16,1024]{1,0:T(8,128)S(1)}, u32[]{:S(2)}, u32[]{:S(2)}) collective-permute-start(f32[16,1024]{1,0:T(8,128)S(1)} %slice_add_fusion), channel_id=1, source_target_pairs={{0,1},{1,2},{2,3},{4,5},{5,6},{6,7},{8,9},{9,10},{10,11},{12,13},{... | collective-permute-start | bytes 196616 | tf_op jit(solution)/shard_map/ppermute | solution.py:22
  274.1 2.3 fusion.5
  276.5 0.0 collective-permute-done.5
  276.5 0.7 fusion.13
  277.3 0.0 collective-permute-done.6
  277.3 0.3 multiply_reduce_fusion
  277.6 6.6 %psum.23 = f32[5,16]{1,0:T(8,128)S(1)} all-reduce(f32[5,16]{1,0:T(8,128)S(1)} %stack.56), channel_id=1, replica_groups=mesh['z'=8,'y'=4,'xl'=2,'xh'=2,'core'=2] {'xh','core'}, use_global_device_ids=true, to_apply=%region_22.23 | all-reduce | flops 80 | bytes 640 | tf_op jit(solution)/shard_map/psum | solution.py:129
  284.2 0.8 add_select_fusion
  (34 shorter events, 0.5 us)
Async XLA Ops:
  7.2 97.0 %reduce-scatter.4.cloned.1.call-start = ((), (), s32[]{:S(2)}) async-start(), calls=%async_computation.3 | async-start | bytes 4718592 | tf_op jit(solution)/shard_map/reduce_scatter | solution.py:96
  10.0 29.7 %collective-permute-start = (bf16[1024,1024]{1,0:T(8,128)(2,1)S(1)}, bf16[1024,1024]{1,0:T(8,128)(2,1)S(1)}, u32[]{:S(2)}, u32[]{:S(2)}) collective-permute-start(bf16[1024,1024]{1,0:T(8,128)(2,1)S(1)} %add_convert_fusion), channel_id=1, source_target_pairs={{1,0},{2,1},{3,2},{5,4},{6,5},{7,6},{9,8},{10,9},{11,10},{13,12},{... | collective-permute-start | bytes 6291464 | tf_op jit(solution)/shard_map/ppermute | solution.py:18
  47.6 82.6 %reduce-scatter.6.cloned.1.call-start = ((), (), s32[]{:S(2)}) async-start(), calls=%async_computation.4 | async-start | bytes 1310720 | tf_op jit(solution)/shard_map/reduce_scatter | solution.py:97
  106.3 61.0 %copy-start.1 = (s32[1024]{0:T(1024)S(1)}, s32[1024]{0:T(1024)}, u32[]{:S(2)}) copy-start(s32[1024]{0:T(1024)} %param.4) | copy-start | bytes 12292
  106.3 61.1 %copy-start = (f32[16,1024]{1,0:T(8,128)S(1)}, f32[16,1024]{1,0:T(8,128)}, u32[]{:S(2)}) copy-start(f32[16,1024]{1,0:T(8,128)} %param.5) | copy-start | bytes 196612
  106.3 44.3 %reduce-scatter.8.cloned.1.call-start = ((), (), s32[]{:S(2)}) async-start(), calls=%async_computation.5 | async-start | bytes 393216 | tf_op jit(solution)/shard_map/reduce_scatter | solution.py:98
  130.3 96.1 %all-gather.8.cloned.1.call-start = ((), (), s32[]{:S(2)}) async-start(), calls=%async_computation.6 | async-start | bytes 4718592 | tf_op jit(solution)/shard_map/all_gather | solution.py:115
  167.3 11.0 %collective-permute-start.1 = (f32[16,1024]{1,0:T(8,128)S(1)}, f32[16,1024]{1,0:T(8,128)S(1)}, u32[]{:S(2)}, u32[]{:S(2)}) collective-permute-start(f32[16,1024]{1,0:T(8,128)S(1)} %get-tuple-element.28), channel_id=1, source_target_pairs={{1,0},{2,1},{3,2},{5,4},{6,5},{7,6},{9,8},{10,9},{11,10},{13,12},{... | collective-permute-start | bytes 196616 | tf_op jit(solution)/shard_map/ppermute | solution.py:18
  226.3 9.9 %copy-start.2 = (bf16[1024,2048]{1,0:T(8,128)(2,1)S(1)}, bf16[1024,2048]{1,0:T(8,128)(2,1)}, u32[]{:S(2)}) copy-start(bf16[1024,2048]{1,0:T(8,128)(2,1)} %all-gather.8.cloned.1.call-done) | copy-start | bytes 12582916
  228.6 8.4 %collective-permute-start.2 = (f32[16,1024]{1,0:T(8,128)S(1)}, f32[16,1024]{1,0:T(8,128)S(1)}, u32[]{:S(2)}, u32[]{:S(2)}) collective-permute-start(f32[16,1024]{1,0:T(8,128)S(1)} %slice_add_fusion.12), channel_id=1, source_target_pairs={{0,1},{1,2},{2,3},{4,5},{5,6},{6,7},{8,9},{9,10},{10,11},{12,13},{... | collective-permute-start | bytes 196616 | tf_op jit(solution)/shard_map/ppermute | solution.py:22
  243.8 12.5 %copy-start.3 = (bf16[1024,2048]{1,0:T(8,128)(2,1)S(1)}, bf16[1024,2048]{1,0:T(8,128)(2,1)}, u32[]{:S(2)}) copy-start(bf16[1024,2048]{1,0:T(8,128)(2,1)} %all-gather.8.cloned.1.call-done) | copy-start | bytes 12582916
  244.0 12.3 %collective-permute-start.3 = (f32[16,1024]{1,0:T(8,128)S(1)}, f32[16,1024]{1,0:T(8,128)S(1)}, u32[]{:S(2)}, u32[]{:S(2)}) collective-permute-start(f32[16,1024]{1,0:T(8,128)S(1)} %get-tuple-element.25), channel_id=1, source_target_pairs={{1,0},{2,1},{3,2},{5,4},{6,5},{7,6},{9,8},{10,9},{11,10},{13,12},{... | collective-permute-start | bytes 196616 | tf_op jit(solution)/shard_map/ppermute | solution.py:18
  249.3 7.8 %collective-permute-start.4 = (f32[16,1024]{1,0:T(8,128)S(1)}, f32[16,1024]{1,0:T(8,128)S(1)}, u32[]{:S(2)}, u32[]{:S(2)}) collective-permute-start(f32[16,1024]{1,0:T(8,128)S(1)} %slice_add_fusion.6), channel_id=1, source_target_pairs={{0,1},{1,2},{2,3},{4,5},{5,6},{6,7},{8,9},{9,10},{10,11},{12,13},{... | collective-permute-start | bytes 196616 | tf_op jit(solution)/shard_map/ppermute | solution.py:22
  264.0 12.5 %copy-start.4 = (bf16[1024,2048]{1,0:T(8,128)(2,1)S(1)}, bf16[1024,2048]{1,0:T(8,128)(2,1)}, u32[]{:S(2)}) copy-start(bf16[1024,2048]{1,0:T(8,128)(2,1)} %all-gather.8.cloned.1.call-done) | copy-start | bytes 12582916
  264.1 12.3 %collective-permute-start.5 = (f32[16,1024]{1,0:T(8,128)S(1)}, f32[16,1024]{1,0:T(8,128)S(1)}, u32[]{:S(2)}, u32[]{:S(2)}) collective-permute-start(f32[16,1024]{1,0:T(8,128)S(1)} %get-tuple-element.19), channel_id=1, source_target_pairs={{1,0},{2,1},{3,2},{5,4},{6,5},{7,6},{9,8},{10,9},{11,10},{13,12},{... | collective-permute-start | bytes 196616 | tf_op jit(solution)/shard_map/ppermute | solution.py:18
  269.5 7.8 %collective-permute-start.6 = (f32[16,1024]{1,0:T(8,128)S(1)}, f32[16,1024]{1,0:T(8,128)S(1)}, u32[]{:S(2)}, u32[]{:S(2)}) collective-permute-start(f32[16,1024]{1,0:T(8,128)S(1)} %slice_add_fusion), channel_id=1, source_target_pairs={{0,1},{1,2},{2,3},{4,5},{5,6},{6,7},{8,9},{9,10},{10,11},{12,13},{... | collective-permute-start | bytes 196616 | tf_op jit(solution)/shard_map/ppermute | solution.py:22
Sparse Core Ops, SparseCore 0:
  47.7 56.3 reduce-scatter.3
  106.7 23.5 reduce-scatter.5
  132.7 17.8 reduce-scatter.7
  167.4 58.8 all-gather.7
where the time goes:
time: 292 us
  waiting for transfers between devices  133 us (46%)
  blocking collectives  79.5 us (27%)
  starting transfers between devices  33.1 us (11%)
  matrix products  23.4 us (8%)
  between operations  14.2 us (5%)
  other arithmetic  8.64 us (3%)
    all_gather x1, waiting for transfers between devices, on_device(): gathered = lax.all_gather(gathered, 'z', axis=0, tiled=True)  48 us
    all_gather x3, blocking collectives, gather_stats(): packed = lax.all_gather(packed, axis, axis=0, tiled=True)  44.3 us
    ppermute x4, waiting for transfers between devices, from_next(): lax.ppermute(block, BLOCK_AXES, [(i + 1, i) for i in range(N_BLOCKS - 1)])  28.8 us
    reduce_scatter x1, waiting for transfers between devices, on_device(): within = lax.psum_scatter(centred, 'z', scatter_dimension=0, tiled=True)  21.1 us
    reduce_scatter x1, waiting for transfers between devices, on_device(): within = lax.psum_scatter(within, 'xl', scatter_dimension=0, tiled=True)  20.2 us
    psum x3, blocking collectives, dots(): return lax.psum(local, BLOCK_AXES)  19.9 us
    ppermute x4, starting transfers between devices, from_next(): lax.ppermute(block, BLOCK_AXES, [(i + 1, i) for i in range(N_BLOCKS - 1)])  18.3 us
    dot_general x9, matrix products, times(): lax.dot_general(split3(vector), matrix, (((1,), (side,)), ((), ())), pref...  15.6 us
  transfers between devices with their start and end apart: 11, of which 6 were waited for; matrix products, arithmetic and copies ran while one was open for 5% of the time, Pallas kernels for 0%

commit v1 on v0

--- a/solution.py
+++ b/solution.py
@@ -126,7 +126,7 @@
 
     def dots(*pairs):
         local = jnp.stack([jnp.sum(a * b, axis=1) for a, b in pairs])
-        return lax.psum(local, BLOCK_AXES)
+        return lax.psum(lax.psum(local, axis_name="xh"), axis_name="core")
 
     mask_row = typed_mask.astype(F32)[None, :]
     right_side = mask_row * z_scores

time: 292 us -> 294 us (level)
  blocking collectives: 79.5 us -> 82.8 us
    psum x3 -> x6, blocking collectives: 19.9 us -> 23.2 us  [dots(): return lax.psum(lax.psum(local, axis_name='xh'), axis_name='core')]
where the time goes in v1:
time: 294 us
  waiting for transfers between devices  133 us (45%)
  blocking collectives  82.8 us (28%)
  starting transfers between devices  32 us (11%)
  matrix products  23.3 us (8%)
  between operations  14.2 us (5%)
  other arithmetic  8.61 us (3%)
    all_gather x1, waiting for transfers between devices, on_device(): gathered = lax.all_gather(gathered, 'z', axis=0, tiled=True)  48 us
    all_gather x3, blocking collectives, gather_stats(): packed = lax.all_gather(packed, axis, axis=0, tiled=True)  44.3 us
    ppermute x4, waiting for transfers between devices, from_next(): lax.ppermute(block, BLOCK_AXES, [(i + 1, i) for i in range(N_BLOCKS - 1)])  28.8 us
    psum x6, blocking collectives, dots(): return lax.psum(lax.psum(local, axis_name='xh'), axis_name='core')  23.2 us
    reduce_scatter x1, waiting for transfers between devices, on_device(): within = lax.psum_scatter(centred, 'z', scatter_dimension=0, tiled=True)  21.1 us
    reduce_scatter x1, waiting for transfers between devices, on_device(): within = lax.psum_scatter(within, 'xl', scatter_dimension=0, tiled=True)  20.2 us
    ppermute x4, starting transfers between devices, from_next(): lax.ppermute(block, BLOCK_AXES, [(i + 1, i) for i in range(N_BLOCKS - 1)])  16.5 us
    dot_general x9, matrix products, times(): lax.dot_general(split3(vector), matrix, (((1,), (side,)), ((), ())), pref...  15.6 us
  transfers between devices with their start and end apart: 11, of which 6 were waited for; matrix products, arithmetic and copies ran while one was open for 5% of the time, Pallas kernels for 0%

profile of v1, /device:TPU:1, one launch (start us, length us, event | category | flops | bytes accessed | tf_op | source)
XLA Modules:
  0.0 293.7 jit_solution(15815478988939840641)
XLA Ops:
  7.2 0.0 reduce-scatter.4.cloned.1.call-start
  7.2 2.8 add_convert_fusion
  10.0 5.1 %collective-permute-start = (bf16[1024,1024]{1,0:T(8,128)(2,1)S(1)}, bf16[1024,1024]{1,0:T(8,128)(2,1)S(1)}, u32[]{:S(2)}, u32[]{:S(2)}) collective-permute-start(bf16[1024,1024]{1,0:T(8,128)(2,1)S(1)} %add_convert_fusion), channel_id=1, source_target_pairs={{1,0},{2,1},{3,2},{5,4},{6,5},{7,6},{9,8},{10,9},{11,10},{13,12},{... | collective-permute-start | bytes 6291464 | tf_op jit(solution)/shard_map/ppermute | solution.py:18
  15.1 24.6 %collective-permute-done = bf16[1024,1024]{1,0:T(8,128)(2,1)S(1)} collective-permute-done((bf16[1024,1024]{1,0:T(8,128)(2,1)S(1)}, bf16[1024,1024]{1,0:T(8,128)(2,1)S(1)}, u32[]{:S(2)}, u32[]{:S(2)}) %collective-permute-start) | collective-permute-done | bytes 2097184 | tf_op jit(solution)/shard_map/ppermute | solution.py:18
  39.7 1.3 convert_reduce_fusion
  41.1 6.4 %subtract_convert_fusion = bf16[1024,2048]{1,0:T(8,128)(2,1)} fusion(f32[2048]{0:T(1024)S(1)} %broadcast_multiply_fusion.3, f32[1024]{0:T(1024)S(1)} %bitcast.95, bf16[1024,1024]{1,0:T(8,128)(2,1)S(1)} %add_convert_fusion, bf16[1024,1024]{1,0:T(8,128)(2,1)S(1)} %collective-permute-done), kind=kOutput, calls=%fused_computation.3 | convolution fusion | flops 4309647360 | bytes 8400896 | tf_op jit(solution)/shard_map/dot_general | solution.py:26
  47.5 0.0 reduce-scatter.4.cloned.1.call-update
  47.5 0.0 reduce-scatter.6.cloned.1.call-start
  47.6 23.4 %all-gather.3 = f32[8,2,2048]{2,1,0:T(2,128)S(1)} all-gather(f32[1,2,2048]{2,1,0:T(2,128)S(1)} %maximum_bitcast_fusion.2), channel_id=2, replica_groups=mesh['z'=8,'y'=4,'xl'=2,'xh'=2,'core'=2] {'z'}, dimensions={0}, use_global_device_ids=true | all-gather | bytes 147456 | tf_op jit(solution)/shard_map/all_gather | solution.py:58
  71.0 0.1 fusion.90
  71.2 11.7 %all-gather.4 = f32[4,9,2048]{2,1,0:T(8,128)S(1)} all-gather(f32[1,9,2048]{2,1,0:T(8,128)S(1)} %maximum_bitcast_fusion.1), channel_id=3, replica_groups=mesh['z'=8,'y'=4,'xl'=2,'xh'=2,'core'=2] {'y'}, dimensions={0}, use_global_device_ids=true | all-gather | bytes 368640 | tf_op jit(solution)/shard_map/all_gather | solution.py:58
  82.9 21.1 %reduce-scatter.4.cloned.1.call-done = bf16[128,2048]{1,0:T(8,128)(2,1)} async-done(((bf16[1024,2048]{1,0:T(8,128)(2,1)}), bf16[128,2048]{1,0:T(8,128)(2,1)}) %reduce-scatter.4.cloned.1.call-update) | async-done | bytes 524304 | tf_op jit(solution)/shard_map/reduce_scatter | solution.py:96
  104.0 2.1 convert_element_type.31
  106.2 0.0 reduce-scatter.6.cloned.1.call-update
  106.2 0.0 reduce-scatter.8.cloned.1.call-start
  106.3 9.2 %all-gather.5 = f32[2,33,2048]{2,1,0:T(8,128)S(1)} all-gather(f32[1,33,2048]{2,1,0:T(8,128)S(1)} %maximum_bitcast_fusion), channel_id=4, replica_groups=mesh['z'=8,'y'=4,'xl'=2,'xh'=2,'core'=2] {'xl'}, dimensions={0}, use_global_device_ids=true | all-gather | bytes 811008 | tf_op jit(solution)/shard_map/all_gather | solution.py:58
  115.5 0.1 slice_reduce_fusion.3
  115.6 0.1 reduce-precision_multiply_fusion.1
  115.7 0.1 reduce-precision_multiply_fusion.2
  115.7 14.4 %reduce-scatter.6.cloned.1.call-done = f32[32,2048]{1,0:T(8,128)} async-done(((f32[128,2048]{1,0:T(8,128)}), f32[32,2048]{1,0:T(8,128)}) %reduce-scatter.6.cloned.1.call-update) | async-done | bytes 262160 | tf_op jit(solution)/shard_map/reduce_scatter | solution.py:97
  130.1 0.0 reduce-scatter.8.cloned.1.call-update
  130.1 0.0 all-gather.8.cloned.1.call-start
  130.2 0.1 fusion.75
  130.3 0.1 fusion.23
  130.3 20.2 %reduce-scatter.8.cloned.1.call-done = f32[16,2048]{1,0:T(8,128)} async-done(((f32[32,2048]{1,0:T(8,128)}), f32[16,2048]{1,0:T(8,128)}) %reduce-scatter.8.cloned.1.call-update) | async-done | bytes 131088 | tf_op jit(solution)/shard_map/reduce_scatter | solution.py:98
  150.5 1.4 fusion.4
  151.9 3.8 %all_gather.21 = bf16[32,2048]{1,0:T(8,128)(2,1)S(1)} all-gather(bf16[16,2048]{1,0:T(8,128)(2,1)S(1)} %fusion.4), channel_id=1, replica_groups=mesh['z'=8,'y'=4,'xl'=2,'xh'=2,'core'=2] {'xl'}, dimensions={0}, use_global_device_ids=true | all-gather | bytes 196608 | tf_op jit(solution)/shard_map/all_gather | solution.py:113
  155.7 11.5 %all_gather.22 = bf16[128,2048]{1,0:T(8,128)(2,1)} all-gather(bf16[32,2048]{1,0:T(8,128)(2,1)S(1)} %all_gather.21), channel_id=1, replica_groups=mesh['z'=8,'y'=4,'xl'=2,'xh'=2,'core'=2] {'y'}, dimensions={0}, use_global_device_ids=true | all-gather | bytes 655360 | tf_op jit(solution)/shard_map/all_gather | solution.py:114
  167.2 0.0 all-gather.8.cloned.1.call-update
  167.3 6.7 %collective-permute-start.1 = (f32[16,1024]{1,0:T(8,128)S(1)}, f32[16,1024]{1,0:T(8,128)S(1)}, u32[]{:S(2)}, u32[]{:S(2)}) collective-permute-start(f32[16,1024]{1,0:T(8,128)S(1)} %get-tuple-element.28), channel_id=1, source_target_pairs={{1,0},{2,1},{3,2},{5,4},{6,5},{7,6},{9,8},{10,9},{11,10},{13,12},{... | collective-permute-start | bytes 196616 | tf_op jit(solution)/shard_map/ppermute | solution.py:18
  174.0 4.2 %collective-permute-done.1 = f32[16,1024]{1,0:T(8,128)S(1)} collective-permute-done((f32[16,1024]{1,0:T(8,128)S(1)}, f32[16,1024]{1,0:T(8,128)S(1)}, u32[]{:S(2)}, u32[]{:S(2)}) %collective-permute-start.1) | collective-permute-done | bytes 65568 | tf_op jit(solution)/shard_map/ppermute | solution.py:18
  178.3 48.0 %all-gather.8.cloned.1.call-done = bf16[1024,2048]{1,0:T(8,128)(2,1)} async-done(((bf16[128,2048]{1,0:T(8,128)(2,1)}), bf16[1024,2048]{1,0:T(8,128)(2,1)}) %all-gather.8.cloned.1.call-update) | async-done | bytes 4194320 | tf_op jit(solution)/shard_map/all_gather | solution.py:115
  226.3 2.2 fusion.19
  228.5 5.3 %collective-permute-start.2 = (f32[16,1024]{1,0:T(8,128)S(1)}, f32[16,1024]{1,0:T(8,128)S(1)}, u32[]{:S(2)}, u32[]{:S(2)}) collective-permute-start(f32[16,1024]{1,0:T(8,128)S(1)} %slice_add_fusion.12), channel_id=1, source_target_pairs={{0,1},{1,2},{2,3},{4,5},{5,6},{6,7},{8,9},{9,10},{10,11},{12,13},{... | collective-permute-start | bytes 196616 | tf_op jit(solution)/shard_map/ppermute | solution.py:22
  233.8 2.3 fusion.9
  236.2 0.7 fusion.21
  237.0 0.0 collective-permute-done.2
  237.0 0.2 multiply_reduce_fusion.10
  237.1 5.3 %psum.42 = f32[2,16]{1,0:T(2,128)S(1)} all-reduce(f32[2,16]{1,0:T(2,128)S(1)} %pad_maximum_fusion.11), channel_id=1, replica_groups=mesh['z'=8,'y'=4,'xl'=2,'xh'=2,'core'=2] {'xh'}, use_global_device_ids=true, to_apply=%region_11.12 | all-reduce | flops 32 | bytes 256 | tf_op jit(solution)/shard_map/psum | solution.py:129
  242.4 2.5 psum.43
  244.9 0.1 reduce-precision_convert_fusion.7
  245.0 2.3 collective-permute-start.3
  247.3 2.1 fusion.15
  249.4 5.0 %collective-permute-start.4 = (f32[16,1024]{1,0:T(8,128)S(1)}, f32[16,1024]{1,0:T(8,128)S(1)}, u32[]{:S(2)}, u32[]{:S(2)}) collective-permute-start(f32[16,1024]{1,0:T(8,128)S(1)} %slice_add_fusion.6), channel_id=1, source_target_pairs={{0,1},{1,2},{2,3},{4,5},{5,6},{6,7},{8,9},{9,10},{10,11},{12,13},{... | collective-permute-start | bytes 196616 | tf_op jit(solution)/shard_map/ppermute | solution.py:22
  254.4 2.3 fusion.7
  256.8 0.0 collective-permute-done.3
  256.8 0.7 fusion.17
  257.6 0.0 collective-permute-done.4
  257.6 0.2 multiply_reduce_fusion.5
  257.8 5.3 %psum.44 = f32[5,16]{1,0:T(8,128)S(1)} all-reduce(f32[5,16]{1,0:T(8,128)S(1)} %stack.50), channel_id=1, replica_groups=mesh['z'=8,'y'=4,'xl'=2,'xh'=2,'core'=2] {'xh'}, use_global_device_ids=true, to_apply=%region_17.18 | all-reduce | flops 80 | bytes 640 | tf_op jit(solution)/shard_map/psum | solution.py:129
  263.1 2.5 psum.45
  265.6 0.1 reduce-precision_convert_fusion.3
  265.7 2.3 collective-permute-start.5
  268.1 2.1 fusion.11
  270.2 5.0 %collective-permute-start.6 = (f32[16,1024]{1,0:T(8,128)S(1)}, f32[16,1024]{1,0:T(8,128)S(1)}, u32[]{:S(2)}, u32[]{:S(2)}) collective-permute-start(f32[16,1024]{1,0:T(8,128)S(1)} %slice_add_fusion), channel_id=1, source_target_pairs={{0,1},{1,2},{2,3},{4,5},{5,6},{6,7},{8,9},{9,10},{10,11},{12,13},{... | collective-permute-start | bytes 196616 | tf_op jit(solution)/shard_map/ppermute | solution.py:22
  275.2 2.3 fusion.5
  277.5 0.0 collective-permute-done.5
  277.5 0.0 copy-done.4
  277.6 0.7 fusion.13
  278.3 0.0 collective-permute-done.6
  278.3 0.3 multiply_reduce_fusion
  278.6 5.3 %psum.46 = f32[5,16]{1,0:T(8,128)S(1)} all-reduce(f32[5,16]{1,0:T(8,128)S(1)} %stack.56), channel_id=1, replica_groups=mesh['z'=8,'y'=4,'xl'=2,'xh'=2,'core'=2] {'xh'}, use_global_device_ids=true, to_apply=%region_24.25 | all-reduce | flops 80 | bytes 640 | tf_op jit(solution)/shard_map/psum | solution.py:129
  283.9 2.5 psum.47
  286.4 0.8 add_select_fusion
  (37 shorter events, 0.5 us)
Async XLA Ops:
  7.2 96.8 %reduce-scatter.4.cloned.1.call-start = ((), (), s32[]{:S(2)}) async-start(), calls=%async_computation.3 | async-start | bytes 4718592 | tf_op jit(solution)/shard_map/reduce_scatter | solution.py:96
  10.0 29.7 %collective-permute-start = (bf16[1024,1024]{1,0:T(8,128)(2,1)S(1)}, bf16[1024,1024]{1,0:T(8,128)(2,1)S(1)}, u32[]{:S(2)}, u32[]{:S(2)}) collective-permute-start(bf16[1024,1024]{1,0:T(8,128)(2,1)S(1)} %add_convert_fusion), channel_id=1, source_target_pairs={{1,0},{2,1},{3,2},{5,4},{6,5},{7,6},{9,8},{10,9},{11,10},{13,12},{... | collective-permute-start | bytes 6291464 | tf_op jit(solution)/shard_map/ppermute | solution.py:18
  47.5 82.6 %reduce-scatter.6.cloned.1.call-start = ((), (), s32[]{:S(2)}) async-start(), calls=%async_computation.4 | async-start | bytes 1310720 | tf_op jit(solution)/shard_map/reduce_scatter | solution.py:97
  106.1 61.1 %copy-start.1 = (s32[1024]{0:T(1024)S(1)}, s32[1024]{0:T(1024)}, u32[]{:S(2)}) copy-start(s32[1024]{0:T(1024)} %param.4) | copy-start | bytes 12292
  106.1 61.1 %copy-start = (f32[16,1024]{1,0:T(8,128)S(1)}, f32[16,1024]{1,0:T(8,128)}, u32[]{:S(2)}) copy-start(f32[16,1024]{1,0:T(8,128)} %param.5) | copy-start | bytes 196612
  106.2 44.4 %reduce-scatter.8.cloned.1.call-start = ((), (), s32[]{:S(2)}) async-start(), calls=%async_computation.5 | async-start | bytes 393216 | tf_op jit(solution)/shard_map/reduce_scatter | solution.py:98
  130.1 96.1 %all-gather.8.cloned.1.call-start = ((), (), s32[]{:S(2)}) async-start(), calls=%async_computation.6 | async-start | bytes 4718592 | tf_op jit(solution)/shard_map/all_gather | solution.py:115
  167.3 11.0 %collective-permute-start.1 = (f32[16,1024]{1,0:T(8,128)S(1)}, f32[16,1024]{1,0:T(8,128)S(1)}, u32[]{:S(2)}, u32[]{:S(2)}) collective-permute-start(f32[16,1024]{1,0:T(8,128)S(1)} %get-tuple-element.28), channel_id=1, source_target_pairs={{1,0},{2,1},{3,2},{5,4},{6,5},{7,6},{9,8},{10,9},{11,10},{13,12},{... | collective-permute-start | bytes 196616 | tf_op jit(solution)/shard_map/ppermute | solution.py:18
  226.3 9.9 %copy-start.2 = (bf16[1024,2048]{1,0:T(8,128)(2,1)S(1)}, bf16[1024,2048]{1,0:T(8,128)(2,1)}, u32[]{:S(2)}) copy-start(bf16[1024,2048]{1,0:T(8,128)(2,1)} %all-gather.8.cloned.1.call-done) | copy-start | bytes 12582916
  228.5 8.4 %collective-permute-start.2 = (f32[16,1024]{1,0:T(8,128)S(1)}, f32[16,1024]{1,0:T(8,128)S(1)}, u32[]{:S(2)}, u32[]{:S(2)}) collective-permute-start(f32[16,1024]{1,0:T(8,128)S(1)} %slice_add_fusion.12), channel_id=1, source_target_pairs={{0,1},{1,2},{2,3},{4,5},{5,6},{6,7},{8,9},{9,10},{10,11},{12,13},{... | collective-permute-start | bytes 196616 | tf_op jit(solution)/shard_map/ppermute | solution.py:22
  244.9 11.9 %copy-start.3 = (bf16[1024,2048]{1,0:T(8,128)(2,1)S(1)}, bf16[1024,2048]{1,0:T(8,128)(2,1)}, u32[]{:S(2)}) copy-start(bf16[1024,2048]{1,0:T(8,128)(2,1)} %all-gather.8.cloned.1.call-done) | copy-start | bytes 12582916
  245.0 11.8 %collective-permute-start.3 = (f32[16,1024]{1,0:T(8,128)S(1)}, f32[16,1024]{1,0:T(8,128)S(1)}, u32[]{:S(2)}, u32[]{:S(2)}) collective-permute-start(f32[16,1024]{1,0:T(8,128)S(1)} %get-tuple-element.25), channel_id=1, source_target_pairs={{1,0},{2,1},{3,2},{5,4},{6,5},{7,6},{9,8},{10,9},{11,10},{13,12},{... | collective-permute-start | bytes 196616 | tf_op jit(solution)/shard_map/ppermute | solution.py:18
  249.4 8.1 %collective-permute-start.4 = (f32[16,1024]{1,0:T(8,128)S(1)}, f32[16,1024]{1,0:T(8,128)S(1)}, u32[]{:S(2)}, u32[]{:S(2)}) collective-permute-start(f32[16,1024]{1,0:T(8,128)S(1)} %slice_add_fusion.6), channel_id=1, source_target_pairs={{0,1},{1,2},{2,3},{4,5},{5,6},{6,7},{8,9},{9,10},{10,11},{12,13},{... | collective-permute-start | bytes 196616 | tf_op jit(solution)/shard_map/ppermute | solution.py:22
  265.6 12.0 %copy-start.4 = (bf16[1024,2048]{1,0:T(8,128)(2,1)S(1)}, bf16[1024,2048]{1,0:T(8,128)(2,1)}, u32[]{:S(2)}) copy-start(bf16[1024,2048]{1,0:T(8,128)(2,1)} %all-gather.8.cloned.1.call-done) | copy-start | bytes 12582916
  265.7 11.8 %collective-permute-start.5 = (f32[16,1024]{1,0:T(8,128)S(1)}, f32[16,1024]{1,0:T(8,128)S(1)}, u32[]{:S(2)}, u32[]{:S(2)}) collective-permute-start(f32[16,1024]{1,0:T(8,128)S(1)} %get-tuple-element.19), channel_id=1, source_target_pairs={{1,0},{2,1},{3,2},{5,4},{6,5},{7,6},{9,8},{10,9},{11,10},{13,12},{... | collective-permute-start | bytes 196616 | tf_op jit(solution)/shard_map/ppermute | solution.py:18
  270.2 8.1 %collective-permute-start.6 = (f32[16,1024]{1,0:T(8,128)S(1)}, f32[16,1024]{1,0:T(8,128)S(1)}, u32[]{:S(2)}, u32[]{:S(2)}) collective-permute-start(f32[16,1024]{1,0:T(8,128)S(1)} %slice_add_fusion), channel_id=1, source_target_pairs={{0,1},{1,2},{2,3},{4,5},{5,6},{6,7},{8,9},{9,10},{10,11},{12,13},{... | collective-permute-start | bytes 196616 | tf_op jit(solution)/shard_map/ppermute | solution.py:22
Sparse Core Ops, SparseCore 0:
  47.6 56.3 reduce-scatter.3
  106.6 23.4 reduce-scatter.5
  132.6 17.9 reduce-scatter.7
  167.3 58.8 all-gather.7
